TPU v7x, 512 devices: a whole 4x8x8 slice. The times are simulated.
512 devices in a mesh: row: 64 (over y, x, core), col: 8 (over z).
Axes of the slice: x: 4, y: 8, z: 8, core: 2. Of those that a mesh axis runs over, the one named last changes fastest.
Arguments:
- hamiltonian: float32 [24576, 24576], P('row', 'col'), as said below
- previous: float32 [24576, 56], P('row', 'col'), may hold values from -6 to 6
- correlation_map: int32 [24576], P('row'), may hold values from 0 to 24575, each once
- lower_cut: float32 [1], replicated, may hold values from 0.5 to 1.5
- upper_bound: float32 [1], replicated, may hold values from 5.5 to 6.5
Outputs:
- basis_out: float32 [24576, 56], P('row', 'col')
- ritz_matrix: float32 [56, 56], replicated
Inputs may be any that keep to these rules, and one draw needn't show every extreme that they name: correlation_map names every index of 0 .. 24575 exactly once. hamiltonian is symmetric.
All inputs are finite; a program needn't handle non-finite values.
Results may differ from a plain program's by a relative error of at most 0.00013.
Values sent between devices are 32-bit elements; how exact they have to be, the bound alone decides.
A program may use at most 64 MiB of HBM per device.

v0:
```python
import jax
import jax.numpy as jnp
from jax import lax
from jax.sharding import PartitionSpec as P

N = 24576
DEG = 4


def body(hamiltonian, previous, correlation_map, lower_cut, upper_bound):
    column_groups = lax.axis_size("col")
    group_width = previous.shape[1]
    width = group_width * column_groups
    centre = (upper_bound[0] + lower_cut[0]) * 0.5
    half_width = (upper_bound[0] - lower_cut[0]) * 0.5
    spread = lax.all_gather(previous, "row", axis=0, tiled=True)
    start_block = jnp.take(spread, correlation_map, axis=0)

    def operate_on(vectors):
        spread_rows = lax.all_gather(vectors, "row", axis=0, tiled=True)
        wanted = lax.all_to_all(spread_rows, "col", split_axis=0, concat_axis=1, tiled=True)
        partial_sum = jnp.dot(hamiltonian, wanted, precision=lax.Precision.HIGHEST)
        return lax.psum_scatter(partial_sum, "col", scatter_dimension=1, tiled=True)

    earlier = start_block
    current = (operate_on(earlier) - centre * earlier) / half_width
    for repeat in range(DEG - 1):
        following = 2.0 * (operate_on(current) - centre * current) / half_width - earlier
        earlier = current
        current = following
    column_index = lax.axis_index("col")
    full_rows = lax.all_gather(current, "col", axis=1, tiled=True)
    empty = jnp.zeros((width, width), jnp.float32)
    block_rows = jnp.dot(current.T, full_rows, precision=lax.Precision.HIGHEST)
    gram_part = lax.dynamic_update_slice_in_dim(empty, block_rows, column_index * group_width, 0)
    gram_total = lax.psum(gram_part, ("row", "col"))
    applied = operate_on(current)
    block_cols = jnp.dot(full_rows.T, applied, precision=lax.Precision.HIGHEST)
    proj_total = lax.psum(
        lax.dynamic_update_slice_in_dim(empty, block_cols, column_index * group_width, 1),
        ("row", "col"),
    )
    gram_matrix = gram_total / N
    projected = proj_total / N
    factor = jnp.linalg.cholesky(gram_matrix)
    identity = jnp.eye(width, dtype=jnp.float32)
    inverse = lax.linalg.triangular_solve(factor, identity, left_side=True, lower=True)
    own_columns = lax.dynamic_slice_in_dim(inverse.T, column_index * group_width, group_width, 1)
    basis_out = jnp.dot(full_rows, own_columns, precision=lax.Precision.HIGHEST)
    ritz_matrix = jnp.dot(
        jnp.dot(inverse, projected, precision=lax.Precision.HIGHEST),
        inverse.T,
        precision=lax.Precision.HIGHEST,
    )
    return (basis_out, ritz_matrix)


def solution(mesh):
    return jax.shard_map(
        body,
        mesh=mesh,
        in_specs=(P("row", "col"), P("row", "col"), P("row"), P(), P()),
        out_specs=(P("row", "col"), P()),
        check_vma=False,
    )
```

profile of v0, /device:TPU:1, one launch (start us, length us, event | category | flops | bytes accessed | tf_op | source)
XLA Modules:
  0.0 1014.7 jit_solution(17210025577529272954)
XLA Ops:
  7.2 0.7 compare_select_fusion
  7.9 0.7 compare_and_fusion
  8.6 0.8 copy.41
  9.4 70.1 %all_gather.21 = f32[24576,7]{1,0:T(8,128)} all-gather(f32[384,7]{1,0:T(8,128)S(1)} %copy.41), channel_id=1, replica_groups=mesh['row'=64,'col'=8] {'row'}, dimensions={0}, use_global_device_ids=true | all-gather | bytes 698880 | tf_op jit(solution)/shard_map/all_gather | solution.py:16
  79.6 5.7 gather_fusion
  85.4 48.9 %all_gather.22 = f32[24576,7]{0,1:T(8,128)S(1)} all-gather(f32[384,7]{0,1:T(8,128)S(1)} %broadcast_select_fusion), channel_id=1, replica_groups=mesh['row'=64,'col'=8] {'row'}, dimensions={0}, use_global_device_ids=true | all-gather | bytes 698880 | tf_op jit(solution)/shard_map/all_gather | solution.py:20
  134.3 30.6 %all_to_all.95 = f32[8,3072,7]{1,2,0:T(8,128)S(1)} all-to-all(f32[8,3072,7]{1,2,0:T(8,128)S(1)} %bitcast.63), channel_id=1, replica_groups=mesh['row'=64,'col'=8] {'col'}, dimensions={0} | all-to-all | bytes 1376256 | tf_op jit(solution)/shard_map/all_to_all | solution.py:21
  164.8 0.1 all_to_all.73
  164.9 7.4 convolution_bitcast_fusion.4
  173.7 1.3 dynamic-slice.4
  175.7 61.5 %all-reduce.12.cloned.1.call-done = f32[384,56]{0,1:T(8,128)} async-done(((f32[384,56]{0,1:T(8,128)}), f32[384,56]{0,1:T(8,128)}) %all-reduce.12.cloned.1.call-update) | async-done | bytes 86032
  237.2 0.7 fusion.18
  237.9 56.2 %all_gather.23 = f32[24576,7]{0,1:T(8,128)S(1)} all-gather(f32[384,7]{0,1:T(8,128)S(1)} %fusion.18), channel_id=1, replica_groups=mesh['row'=64,'col'=8] {'row'}, dimensions={0}, use_global_device_ids=true | all-gather | bytes 698880 | tf_op jit(solution)/shard_map/all_gather | solution.py:20
  294.1 28.4 %all_to_all.96 = f32[8,3072,7]{1,2,0:T(8,128)S(1)} all-to-all(f32[8,3072,7]{1,2,0:T(8,128)S(1)} %bitcast.68), channel_id=1, replica_groups=mesh['row'=64,'col'=8] {'col'}, dimensions={0} | all-to-all | bytes 1376256 | tf_op jit(solution)/shard_map/all_to_all | solution.py:21
  322.5 0.1 all_to_all.77
  322.6 7.4 convolution_bitcast_fusion.3
  330.1 64.8 %all-reduce.14.cloned.1.call-done = f32[384,56]{0,1:T(8,128)} async-done(((f32[384,56]{0,1:T(8,128)}), f32[384,56]{0,1:T(8,128)}) %all-reduce.14.cloned.1.call-update) | async-done | bytes 86032
  394.9 0.7 fusion.17
  395.6 55.7 %all_gather.24 = f32[24576,7]{0,1:T(8,128)S(1)} all-gather(f32[384,7]{0,1:T(8,128)S(1)} %fusion.17), channel_id=1, replica_groups=mesh['row'=64,'col'=8] {'row'}, dimensions={0}, use_global_device_ids=true | all-gather | bytes 698880 | tf_op jit(solution)/shard_map/all_gather | solution.py:20
  451.4 28.6 %all_to_all.97 = f32[8,3072,7]{1,2,0:T(8,128)S(1)} all-to-all(f32[8,3072,7]{1,2,0:T(8,128)S(1)} %bitcast.69), channel_id=1, replica_groups=mesh['row'=64,'col'=8] {'col'}, dimensions={0} | all-to-all | bytes 1376256 | tf_op jit(solution)/shard_map/all_to_all | solution.py:21
  479.9 0.1 all_to_all.81
  480.0 7.5 convolution_bitcast_fusion.2
  487.5 64.9 %all-reduce.16.cloned.1.call-done = f32[384,56]{0,1:T(8,128)} async-done(((f32[384,56]{0,1:T(8,128)}), f32[384,56]{0,1:T(8,128)}) %all-reduce.16.cloned.1.call-update) | async-done | bytes 86032
  552.4 0.7 fusion.14
  553.2 55.7 %all_gather.25 = f32[24576,7]{0,1:T(8,128)S(1)} all-gather(f32[384,7]{0,1:T(8,128)S(1)} %fusion.14), channel_id=1, replica_groups=mesh['row'=64,'col'=8] {'row'}, dimensions={0}, use_global_device_ids=true | all-gather | bytes 698880 | tf_op jit(solution)/shard_map/all_gather | solution.py:20
  608.8 28.4 %all_to_all.98 = f32[8,3072,7]{1,2,0:T(8,128)S(1)} all-to-all(f32[8,3072,7]{1,2,0:T(8,128)S(1)} %bitcast.70), channel_id=1, replica_groups=mesh['row'=64,'col'=8] {'col'}, dimensions={0} | all-to-all | bytes 1376256 | tf_op jit(solution)/shard_map/all_to_all | solution.py:21
  637.3 7.5 convolution_bitcast_fusion.1
  644.8 64.9 %all-reduce.18.cloned.1.call-done = f32[384,56]{0,1:T(8,128)} async-done(((f32[384,56]{0,1:T(8,128)}), f32[384,56]{0,1:T(8,128)}) %all-reduce.18.cloned.1.call-update) | async-done | bytes 86032
  709.7 0.7 fusion.11
  710.4 60.3 %all_gather.27 = f32[24576,7]{0,1:T(8,128)} all-gather(f32[384,7]{0,1:T(8,128)S(1)} %fusion.11), channel_id=1, replica_groups=mesh['row'=64,'col'=8] {'row'}, dimensions={0}, use_global_device_ids=true | all-gather | bytes 698880 | tf_op jit(solution)/shard_map/all_gather | solution.py:20
  770.7 5.1 all-to-all-start.4
  775.8 33.0 %all-gather = f32[8,7,384]{2,1,0:T(8,128)S(1)} all-gather(f32[1,7,384]{2,1,0:T(8,128)S(1)} %bitcast.71), channel_id=1, replica_groups=mesh['row'=64,'col'=8] {'col'}, dimensions={0}, use_global_device_ids=true | all-gather | bytes 96768 | tf_op jit(solution)/shard_map/all_gather | solution.py:32
  808.8 0.1 all_to_all.89
  808.9 7.4 convolution_bitcast_fusion
  816.4 0.2 fusion.24
  816.6 0.1 dynamic_update_slice.6
  816.7 74.4 %all-reduce.20.cloned.1.call-done = f32[384,56]{0,1:T(8,128)} async-done(((f32[384,56]{0,1:T(8,128)}), f32[384,56]{0,1:T(8,128)}) %all-reduce.20.cloned.1.call-update) | async-done | bytes 86032
  891.1 1.0 fusion.7
  892.1 0.3 dynamic_update_slice.7
  892.4 102.7 %all-reduce.5 = (f32[56,56]{1,0:T(8,128)S(1)}, f32[56,56]{1,0:T(8,128)S(1)}) all-reduce(f32[56,56]{1,0:T(8,128)S(1)} %dynamic_update_slice.6, f32[56,56]{1,0:T(8,128)S(1)} %dynamic_update_slice.7), channel_id=1, replica_groups=mesh['row'=64,'col'=8] {'row','col'}, use_global_device_ids=true, to_apply=%region_4.5 | all-reduce | flops 6272 | bytes 50176 | tf_op jit(solution)/shard_map/psum | solution.py:36
  995.2 5.1 cholesky.16
  1000.3 0.6 compare_reduce_fusion
  1001.0 0.7 fusion
  1001.6 4.3 custom-call.6
  1005.9 0.2 fusion.1
  1006.2 0.8 fusion.19
  1006.9 0.2 fusion.4
  1007.1 0.8 fusion.25
  (22 shorter events, 0.6 us)
Async XLA Ops:
  7.2 230.0 %all-reduce.12.cloned.1.call-start = ((), (), s32[]{:S(2)}) async-start(), calls=%async_computation.5 | async-start | bytes 172032
  172.4 222.5 %all-reduce.14.cloned.1.call-start = ((), (), s32[]{:S(2)}) async-start(), calls=%async_computation.6 | async-start | bytes 172032
  330.0 222.4 %all-reduce.16.cloned.1.call-start = ((), (), s32[]{:S(2)}) async-start(), calls=%async_computation.7 | async-start | bytes 172032
  487.5 222.2 %all-reduce.18.cloned.1.call-start = ((), (), s32[]{:S(2)}) async-start(), calls=%async_computation.8 | async-start | bytes 172032
  770.7 38.1 %all-to-all-start.4 = ((f32[8,3072,7]{1,2,0:T(8,128)}), f32[8,3072,7]{1,2,0:T(8,128)S(1)}, u32[]{:S(2)}, u32[]{:S(2)}) async-start(f32[8,3072,7]{1,2,0:T(8,128)} %bitcast.19), calls=%async_computation.4 | async-start | bytes 1572864 | tf_op jit(solution)/shard_map/all_to_all | solution.py:21
  775.8 115.3 %all-reduce.20.cloned.1.call-start = ((), (), s32[]{:S(2)}) async-start(), calls=%async_computation.9 | async-start | bytes 172032
Sparse Core Ops, SparseCore 0:
  172.5 64.5 all-reduce.11
  330.2 64.6 all-reduce.13
  487.6 64.7 all-reduce.15
  644.9 64.7 all-reduce.17
  816.5 74.5 all-reduce.19
where the time goes:
time: 1020 us; the launch traced here: 1010 us
  blocking collectives  598 us (59%)
  waiting for transfers between devices  330 us (32%)
  matrix products  40.4 us (4%)
  between operations  16.1 us (2%)
  other arithmetic  15.1 us (1%)
    unnamed x10, waiting for transfers between devices  330 us
    all_gather x5, blocking collectives, operate_on(): spread_rows = lax.all_gather(vectors, 'row', axis=0, tiled=True)  277 us
    all_to_all x4, blocking collectives, operate_on(): lax.all_to_all(spread_rows, 'col', split_axis=0, concat_axis=1, tiled=True)  116 us
    psum x1, blocking collectives, body(): gram_total = lax.psum(gram_part, ('row', 'col'))  103 us
    all_gather x1, blocking collectives, body(): spread = lax.all_gather(previous, 'row', axis=0, tiled=True)  70.1 us
    dot_general x5, matrix products, operate_on(): partial_sum = jnp.dot(hamiltonian, wanted, precision=lax.Precision.HIGHEST)  37.2 us
    all_gather x1, blocking collectives, body(): full_rows = lax.all_gather(current, 'col', axis=1, tiled=True)  33 us
  transfers between devices with their start and end apart: 6, of which 5 were waited for; matrix products, arithmetic and copies ran while one was open for 0% of the time, Pallas kernels for 0%

commit v1 on v0

--- a/solution.py
+++ b/solution.py
@@ -29,7 +29,13 @@
         earlier = current
         current = following
     column_index = lax.axis_index("col")
-    full_rows = lax.all_gather(current, "col", axis=1, tiled=True)
+    devices = lax.axis_size("col")
+    current_2, pieces = (current, [current])
+    for _ in range(devices - 1):
+        current_2 = lax.ppermute(current_2, "col", [(i, (i + 1) % devices) for i in range(devices)])
+        pieces.insert(0, current_2)
+    row_of_blocks = jnp.concatenate(pieces, axis=1)
+    full_rows = jnp.roll(row_of_blocks, (lax.axis_index("col") + 1) * current.shape[1], axis=1)
     empty = jnp.zeros((width, width), jnp.float32)
     block_rows = jnp.dot(current.T, full_rows, precision=lax.Precision.HIGHEST)
     gram_part = lax.dynamic_update_slice_in_dim(empty, block_rows, column_index * group_width, 0)

time: 1020 us -> 1050 us (1.029)
  waiting for transfers between devices: 330 us -> 369 us
  blocking collectives: 598 us -> 566 us
  starting transfers between devices: 5.3 us -> 21.1 us
    ppermute x0 -> x7, waiting for transfers between devices: none -> 35 us  [body(): lax.ppermute(current_2, 'col', [(i, (i + 1) % devices) for i in range(dev...]
    all_gather x1 -> x0, blocking collectives: 33 us -> none  [body(): full_rows = lax.all_gather(current, 'col', axis=1, tiled=True)]
    ppermute x0 -> x7, starting transfers between devices: none -> 15.8 us  [body(): lax.ppermute(current_2, 'col', [(i, (i + 1) % devices) for i in range(dev...]
  transfers between devices with their start and end apart: 6 -> 13, of which waited for: 5 -> 12; matrix products, arithmetic and copies ran while one was open for 0% -> 0% of each run, Pallas kernels for 0% -> 0%
where the time goes in v1:
time: 1050 us; the launch traced here: 1040 us
  blocking collectives  566 us (54%)
  waiting for transfers between devices  369 us (35%)
  matrix products  40.4 us (4%)
  starting transfers between devices  21.1 us (2%)
  between operations  16.2 us (2%)
  other arithmetic  15.1 us (1%)
    unnamed x10, waiting for transfers between devices  334 us
    all_gather x5, blocking collectives, operate_on(): spread_rows = lax.all_gather(vectors, 'row', axis=0, tiled=True)  277 us
    all_to_all x4, blocking collectives, operate_on(): lax.all_to_all(spread_rows, 'col', split_axis=0, concat_axis=1, tiled=True)  116 us
    psum x1, blocking collectives, body(): gram_total = lax.psum(gram_part, ('row', 'col'))  103 us
    all_gather x1, blocking collectives, body(): spread = lax.all_gather(previous, 'row', axis=0, tiled=True)  70.1 us
    dot_general x5, matrix products, operate_on(): partial_sum = jnp.dot(hamiltonian, wanted, precision=lax.Precision.HIGHEST)  37.2 us
    ppermute x7, waiting for transfers between devices, body(): lax.ppermute(current_2, 'col', [(i, (i + 1) % devices) for i in range(dev...  35 us
  transfers between devices with their start and end apart: 13, of which 12 were waited for; matrix products, arithmetic and copies ran while one was open for 0% of the time, Pallas kernels for 0%

profile of v1, /device:TPU:1, one launch (start us, length us, event | category | flops | bytes accessed | tf_op | source)
XLA Modules:
  0.0 1037.8 jit_solution(10930689066398907103)
XLA Ops:
  8.6 0.8 copy.40
  9.4 70.1 %all_gather.18 = f32[24576,7]{1,0:T(8,128)} all-gather(f32[384,7]{1,0:T(8,128)S(1)} %copy.40), channel_id=1, replica_groups=mesh['row'=64,'col'=8] {'row'}, dimensions={0}, use_global_device_ids=true | all-gather | bytes 698880 | tf_op jit(solution)/shard_map/all_gather | solution.py:16
  79.6 5.7 gather_fusion
  85.4 48.9 %all_gather.19 = f32[24576,7]{0,1:T(8,128)S(1)} all-gather(f32[384,7]{0,1:T(8,128)S(1)} %broadcast_select_fusion), channel_id=1, replica_groups=mesh['row'=64,'col'=8] {'row'}, dimensions={0}, use_global_device_ids=true | all-gather | bytes 698880 | tf_op jit(solution)/shard_map/all_gather | solution.py:20
  134.3 30.6 %all_to_all.95 = f32[8,3072,7]{1,2,0:T(8,128)S(1)} all-to-all(f32[8,3072,7]{1,2,0:T(8,128)S(1)} %bitcast.57), channel_id=1, replica_groups=mesh['row'=64,'col'=8] {'col'}, dimensions={0} | all-to-all | bytes 1376256 | tf_op jit(solution)/shard_map/all_to_all | solution.py:21
  164.9 7.4 convolution_bitcast_fusion.4
  173.7 1.3 dynamic-slice.4
  175.7 61.5 %all-reduce.12.cloned.1.call-done = f32[384,56]{0,1:T(8,128)} async-done(((f32[384,56]{0,1:T(8,128)}), f32[384,56]{0,1:T(8,128)}) %all-reduce.12.cloned.1.call-update) | async-done | bytes 86032
  237.2 0.7 fusion.23
  237.9 56.2 %all_gather.20 = f32[24576,7]{0,1:T(8,128)S(1)} all-gather(f32[384,7]{0,1:T(8,128)S(1)} %fusion.23), channel_id=1, replica_groups=mesh['row'=64,'col'=8] {'row'}, dimensions={0}, use_global_device_ids=true | all-gather | bytes 698880 | tf_op jit(solution)/shard_map/all_gather | solution.py:20
  294.1 28.4 %all_to_all.96 = f32[8,3072,7]{1,2,0:T(8,128)S(1)} all-to-all(f32[8,3072,7]{1,2,0:T(8,128)S(1)} %bitcast.62), channel_id=1, replica_groups=mesh['row'=64,'col'=8] {'col'}, dimensions={0} | all-to-all | bytes 1376256 | tf_op jit(solution)/shard_map/all_to_all | solution.py:21
  322.6 7.4 convolution_bitcast_fusion.3
  330.1 64.8 %all-reduce.14.cloned.1.call-done = f32[384,56]{0,1:T(8,128)} async-done(((f32[384,56]{0,1:T(8,128)}), f32[384,56]{0,1:T(8,128)}) %all-reduce.14.cloned.1.call-update) | async-done | bytes 86032
  395.6 55.7 %all_gather.21 = f32[24576,7]{0,1:T(8,128)S(1)} all-gather(f32[384,7]{0,1:T(8,128)S(1)} %fusion.22), channel_id=1, replica_groups=mesh['row'=64,'col'=8] {'row'}, dimensions={0}, use_global_device_ids=true | all-gather | bytes 698880 | tf_op jit(solution)/shard_map/all_gather | solution.py:20
  451.3 28.6 %all_to_all.97 = f32[8,3072,7]{1,2,0:T(8,128)S(1)} all-to-all(f32[8,3072,7]{1,2,0:T(8,128)S(1)} %bitcast.63), channel_id=1, replica_groups=mesh['row'=64,'col'=8] {'col'}, dimensions={0} | all-to-all | bytes 1376256 | tf_op jit(solution)/shard_map/all_to_all | solution.py:21
  480.0 7.5 convolution_bitcast_fusion.2
  487.5 64.8 %all-reduce.16.cloned.1.call-done = f32[384,56]{0,1:T(8,128)} async-done(((f32[384,56]{0,1:T(8,128)}), f32[384,56]{0,1:T(8,128)}) %all-reduce.16.cloned.1.call-update) | async-done | bytes 86032
  552.4 0.7 fusion.19
  553.1 55.7 %all_gather.22 = f32[24576,7]{0,1:T(8,128)S(1)} all-gather(f32[384,7]{0,1:T(8,128)S(1)} %fusion.19), channel_id=1, replica_groups=mesh['row'=64,'col'=8] {'row'}, dimensions={0}, use_global_device_ids=true | all-gather | bytes 698880 | tf_op jit(solution)/shard_map/all_gather | solution.py:20
  608.8 28.4 %all_to_all.98 = f32[8,3072,7]{1,2,0:T(8,128)S(1)} all-to-all(f32[8,3072,7]{1,2,0:T(8,128)S(1)} %bitcast.64), channel_id=1, replica_groups=mesh['row'=64,'col'=8] {'col'}, dimensions={0} | all-to-all | bytes 1376256 | tf_op jit(solution)/shard_map/all_to_all | solution.py:21
  637.3 7.4 convolution_bitcast_fusion.1
  644.7 64.8 %all-reduce.18.cloned.1.call-done = f32[384,56]{0,1:T(8,128)} async-done(((f32[384,56]{0,1:T(8,128)}), f32[384,56]{0,1:T(8,128)}) %all-reduce.18.cloned.1.call-update) | async-done | bytes 86032
  709.5 0.7 fusion.16
  710.3 60.6 %all_gather.23 = f32[24576,7]{0,1:T(8,128)} all-gather(f32[384,7]{0,1:T(8,128)S(1)} %fusion.16), channel_id=1, replica_groups=mesh['row'=64,'col'=8] {'row'}, dimensions={0}, use_global_device_ids=true | all-gather | bytes 698880 | tf_op jit(solution)/shard_map/all_gather | solution.py:20
  770.9 5.1 all-to-all-start.4
  776.0 3.3 collective-permute-start
  779.3 12.8 %collective-permute-done = f32[384,7]{0,1:T(8,128)S(1)} collective-permute-done((f32[384,7]{0,1:T(8,128)S(1)}, f32[384,7]{0,1:T(8,128)S(1)}, u32[]{:S(2)}, u32[]{:S(2)}) %collective-permute-start) | collective-permute-done | bytes 10784 | tf_op jit(solution)/shard_map/ppermute | solution.py:35
  792.1 2.9 collective-permute-start.1
  795.0 3.7 collective-permute-done.1
  798.7 2.0 collective-permute-start.2
  800.7 3.7 collective-permute-done.2
  804.4 1.9 collective-permute-start.3
  806.3 3.7 collective-permute-done.3
  810.0 1.9 collective-permute-start.4
  811.9 3.7 collective-permute-done.4
  815.6 1.9 collective-permute-start.5
  817.6 3.7 collective-permute-done.5
  821.3 1.9 collective-permute-start.6
  823.2 3.7 collective-permute-done.6
  826.9 1.1 concatenate.6
  828.2 7.4 convolution_bitcast_fusion
  836.0 78.2 %all-reduce.20.cloned.1.call-done = f32[384,56]{0,1:T(8,128)} async-done(((f32[384,56]{0,1:T(8,128)}), f32[384,56]{0,1:T(8,128)}) %all-reduce.20.cloned.1.call-update) | async-done | bytes 86032
  914.2 1.0 fusion
  915.5 102.7 %all-reduce.5 = (f32[56,56]{1,0:T(8,128)S(1)}, f32[56,56]{1,0:T(8,128)S(1)}) all-reduce(f32[56,56]{1,0:T(8,128)S(1)} %dynamic_update_slice.6, f32[56,56]{1,0:T(8,128)S(1)} %dynamic_update_slice.7), channel_id=1, replica_groups=mesh['row'=64,'col'=8] {'row','col'}, use_global_device_ids=true, to_apply=%region_4.5 | all-reduce | flops 6272 | bytes 50176 | tf_op jit(solution)/shard_map/psum | solution.py:42
  1018.2 5.1 cholesky.16
  1024.7 4.3 custom-call.6
  1029.2 0.8 fusion.2
  1030.2 0.8 fusion.30
  (35 shorter events, 5.5 us)
Async XLA Ops:
  7.2 230.0 %all-reduce.12.cloned.1.call-start = ((), (), s32[]{:S(2)}) async-start(), calls=%async_computation.5 | async-start | bytes 172032
  172.4 222.5 %all-reduce.14.cloned.1.call-start = ((), (), s32[]{:S(2)}) async-start(), calls=%async_computation.6 | async-start | bytes 172032
  330.1 222.3 %all-reduce.16.cloned.1.call-start = ((), (), s32[]{:S(2)}) async-start(), calls=%async_computation.7 | async-start | bytes 172032
  487.5 222.1 %all-reduce.18.cloned.1.call-start = ((), (), s32[]{:S(2)}) async-start(), calls=%async_computation.8 | async-start | bytes 172032
  770.9 57.2 %all-to-all-start.4 = ((f32[8,3072,7]{1,2,0:T(8,128)}), f32[8,3072,7]{1,2,0:T(8,128)S(1)}, u32[]{:S(2)}, u32[]{:S(2)}) async-start(f32[8,3072,7]{1,2,0:T(8,128)} %bitcast.17), calls=%async_computation.4 | async-start | bytes 1572864 | tf_op jit(solution)/shard_map/all_to_all | solution.py:21
  776.0 138.2 %all-reduce.20.cloned.1.call-start = ((), (), s32[]{:S(2)}) async-start(), calls=%async_computation.9 | async-start | bytes 172032
  776.0 16.1 %collective-permute-start = (f32[384,7]{0,1:T(8,128)S(1)}, f32[384,7]{0,1:T(8,128)S(1)}, u32[]{:S(2)}, u32[]{:S(2)}) collective-permute-start(f32[384,7]{0,1:T(8,128)S(1)} %fusion.16), channel_id=1, source_target_pairs={{0,1},{1,2},{2,3},{3,4},{4,5},{5,6},{6,7},{7,0},{8,9},{9,10},{10,1... | collective-permute-start | bytes 32264 | tf_op jit(solution)/shard_map/ppermute | solution.py:35
  792.1 6.6 collective-permute-start.1
  798.7 5.6 collective-permute-start.2
  804.4 5.6 collective-permute-start.3
  810.0 5.6 collective-permute-start.4
  815.6 5.6 collective-permute-start.5
  821.3 5.6 collective-permute-start.6
Sparse Core Ops, SparseCore 0:
  172.5 64.5 all-reduce.11
  330.2 64.6 all-reduce.13
  487.6 64.7 all-reduce.15
  644.9 64.6 all-reduce.17
  835.8 78.3 all-reduce.19
